TPU v7x, 512 devices: a whole 4x4x16 slice. The times are simulated.
512 devices in a mesh: tm: 128 (over z, y, core), mod: 4 (over x).
Axes of the slice: x: 4, y: 4, z: 16, core: 2. Of those that a mesh axis runs over, the one named last changes fastest.
Arguments:
- filterbank: bfloat16 [16384, 128], P('tm'), may hold values from -6 to 6
- conv_weight: bfloat16 [384, 1280], replicated, may hold values from -0.3125 to 0.3125
- mlp_gain: float32 [1280], replicated, may hold values from 0.25 to 1.75
- up_weight: bfloat16 [1280, 5120], P('tm', 'mod'), may hold values from -0.15625 to 0.15625
- down_weight: bfloat16 [5120, 1280], P('mod', 'tm'), may hold values from -0.078125 to 0.078125
- post_gain: float32 [1280], replicated, may hold values from 0.25 to 1.75
- audio_weight: bfloat16 [1280, 1792], P(None, 'mod'), may hold values from -0.15625 to 0.15625
- patches: bfloat16 [32768, 1280], P('tm'), may hold values from -6 to 6
- vision_gain: float32 [1280], replicated, may hold values from 0.25 to 1.75
- vision_weight: bfloat16 [5120, 1792], P('tm', 'mod'), may hold values from -0.078125 to 0.078125
- retention: int32 [128, 64], P('tm'), may hold values from 0 to 63, each once within a row
- kept_count: int32 [128], P('tm'), may hold values from 1 to 64, 4096 in all
Outputs:
- sequence: bfloat16 [128, 96, 1792], P('tm', None, 'mod')
Inputs may be any that keep to these rules, and one draw needn't show every extreme that they name: `retention`: each row lists every merged token of its frame once. `kept_count`: the counts sum to 4096.
All inputs are finite; a program needn't handle non-finite values. No bound on the sum of `kept_count` on one device may be relied on, other than what follows from the above.
Results may differ from a plain program's by a relative error of at most 0.01.
Values may be sent and summed in bfloat16 or wider, within the bound.
No kernel may reach another device: no remote copies, remote signals or barrier semaphores. Data moves between devices by JAX's collectives and lax.ppermute only.
A program may use at most 64 MiB of HBM per device.

v0:
```python
import jax
import jax.numpy as jnp
from jax import lax
from jax.sharding import PartitionSpec as P

MRG_FRAME = 64
AUD_TOK = 64
SEQ_DEV = 96


def carried_in(value, axis, join, neutral):
    count, mine = (lax.axis_size(axis), lax.axis_index(axis))
    pieces = lax.all_gather(value, axis)
    running = jnp.full_like(value, 0) + jnp.asarray(neutral, value.dtype)

    def hop(position, running):
        longer = join(running, pieces[position])
        return jnp.where(position < mine, longer, running)

    return lax.fori_loop(0, count - 1, hop, running)


def padded(shard, sides, width):
    for axis, dim in sides:
        peers, length = (lax.axis_size(axis), shard.shape[dim])
        up = [(i, (i + 1) % peers) for i in range(peers - 1)]
        down = [(j, i) for i, j in up]
        last = lax.slice_in_dim(shard, length - width, length, axis=dim)
        first = lax.slice_in_dim(shard, 0, width, axis=dim)
        before = lax.ppermute(last, axis, up)
        after = lax.ppermute(first, axis, down)
        shard = jnp.concatenate([before, shard, after], axis=dim)
    return shard


def layer_norm(values, scale_gain):
    average = jnp.mean(values, axis=-1, keepdims=True)
    centred = values - average
    variance = jnp.mean(centred * centred, axis=-1, keepdims=True)
    return centred * lax.rsqrt(variance + 1e-05) * scale_gain


def rms_norm(values, scale_gain):
    square_mean = jnp.mean(values * values, axis=-1, keepdims=True)
    return values * lax.rsqrt(square_mean + 1e-06) * scale_gain


def pool_pairs(values):
    return values.reshape(-1, 2, values.shape[-1]).mean(axis=1)


def add_counts(earlier, later):
    return earlier + later


def on_device(
    filterbank,
    conv_weight,
    mlp_gain,
    up_weight,
    down_weight,
    post_gain,
    audio_weight,
    patches,
    vision_gain,
    vision_weight,
    retention,
    kept_count,
):
    placed = kept_count + AUD_TOK
    starts = carried_in(placed, "tm", add_counts, jnp.zeros((1,), jnp.int32))
    framed = padded(filterbank, (("tm", 0),), 1)
    unfolded = jnp.concatenate([framed[:-2], framed[1:-1], framed[2:]], axis=1)
    stem = jax.nn.gelu(
        jnp.dot(unfolded, conv_weight, preferred_element_type=jnp.float32), approximate=False
    ).astype(jnp.bfloat16)
    residual = stem.astype(jnp.float32)
    hidden = layer_norm(residual, mlp_gain).astype(jnp.bfloat16)
    up_share = lax.all_gather(up_weight, "tm", axis=0, tiled=True)
    pre_act = jnp.dot(hidden, up_share, preferred_element_type=jnp.float32)
    activated = jax.nn.gelu(pre_act, approximate=False).astype(jnp.bfloat16)
    down_share = lax.all_gather(down_weight, "tm", axis=1, tiled=True)
    partial_value = jnp.dot(activated, down_share, preferred_element_type=jnp.float32)
    summed = lax.psum(partial_value.astype(jnp.bfloat16), "mod").astype(jnp.float32)
    pooled = pool_pairs(residual + summed)
    normed = layer_norm(pooled, post_gain).astype(jnp.bfloat16)
    audio_tokens = jnp.dot(normed, audio_weight, preferred_element_type=jnp.float32).astype(
        jnp.bfloat16
    )
    patch_normed = rms_norm(patches.astype(jnp.float32), vision_gain).astype(jnp.bfloat16)
    merged = patch_normed.reshape(-1, 4 * patch_normed.shape[1])
    vision_share = lax.all_gather(vision_weight, "tm", axis=0, tiled=True)
    visual_tokens = jnp.dot(merged, vision_share, preferred_element_type=jnp.float32).astype(
        jnp.bfloat16
    )
    peer_count = lax.axis_size("tm")
    per_peer = (AUD_TOK + MRG_FRAME + peer_count - 1) // peer_count
    kept_here = kept_count[0]
    first_slot = starts[0]
    all_tokens = jnp.concatenate([visual_tokens, audio_tokens], axis=0)
    peer_ids = jnp.arange(peer_count, dtype=jnp.int32)[:, None]
    round_ids = jnp.arange(per_peer, dtype=jnp.int32)[None, :]
    local_index = round_ids * peer_count + (peer_ids - first_slot) % peer_count
    valid_rows = local_index < kept_here + AUD_TOK
    kept_index = jnp.take(retention[0], jnp.minimum(local_index, MRG_FRAME - 1), axis=0)
    source_index = jnp.where(
        local_index < kept_here, kept_index, MRG_FRAME + local_index - kept_here
    )
    source_index = jnp.where(valid_rows, source_index, 0).astype(jnp.int32)
    send_rows = jnp.take(all_tokens, source_index.reshape(-1), axis=0).reshape(
        peer_count, per_peer, all_tokens.shape[1]
    )
    send_slots = jnp.where(valid_rows, (first_slot + local_index) // peer_count, SEQ_DEV).astype(
        jnp.int32
    )
    recv_rows, recv_slots = (
        lax.all_to_all(send_rows, "tm", split_axis=0, concat_axis=0, tiled=True),
        lax.all_to_all(send_slots, "tm", split_axis=0, concat_axis=0, tiled=True),
    )
    sequence = jnp.zeros((SEQ_DEV, all_tokens.shape[1]), jnp.bfloat16)
    sequence = sequence.at[recv_slots.reshape(-1)].set(
        recv_rows.reshape(-1, all_tokens.shape[1]), mode="drop"
    )
    return sequence[None]


def solution(mesh):
    return jax.shard_map(
        on_device,
        mesh=mesh,
        in_specs=(
            P("tm", None),
            P(),
            P(),
            P("tm", "mod"),
            P("mod", "tm"),
            P(),
            P(None, "mod"),
            P("tm", None),
            P(),
            P("tm", "mod"),
            P("tm", None),
            P("tm"),
        ),
        out_specs=P("tm", None, "mod"),
        check_vma=False,
    )
```

profile of v0, /device:TPU:33, one launch (start us, length us, event | category | flops | bytes accessed | tf_op | source)
XLA Modules:
  0.0 566.4 jit_solution(12969941539579024190)
XLA Ops:
  6.5 0.7 all-gather.9.cloned.1.call-update
  7.3 0.7 all-gather.11.cloned.1.call-update
  8.1 0.7 fusion.127
  8.8 3.8 collective-permute-start
  12.5 1.9 collective-permute-start.1
  14.5 2.9 collective-permute-done.1
  17.4 3.0 convert_reduce_fusion
  20.6 137.2 %all-gather.9.cloned.1.call-done = bf16[128,10,1280]{2,1,0:T(8,128)(2,1)} async-done(((bf16[1,10,1280]{2,1,0:T(8,128)(2,1)}), bf16[128,10,1280]{2,1,0:T(8,128)(2,1)}) %all-gather.9.cloned.1.call-update) | async-done | bytes 3276816 | tf_op jit(solution)/shard_map/all_gather | solution.py:79
  157.8 7.0 %reshape.396 = bf16[1280,1280]{1,0:T(8,128)(2,1)} reshape(bf16[128,10,1280]{2,1,0:T(8,128)(2,1)} %all-gather.9.cloned.1.call-done) | data formatting | bytes 6553600
  164.9 134.5 %all-gather.11.cloned.1.call-done = bf16[128,10,1280]{2,1,0:T(8,128)(2,1)} async-done(((bf16[1,10,1280]{2,1,0:T(8,128)(2,1)}), bf16[128,10,1280]{2,1,0:T(8,128)(2,1)}) %all-gather.11.cloned.1.call-update) | async-done | bytes 3276816 | tf_op jit(solution)/shard_map/all_gather | solution.py:82
  299.4 7.0 %reshape.398 = bf16[1280,1280]{1,0:T(8,128)(2,1)} reshape(bf16[128,10,1280]{2,1,0:T(8,128)(2,1)} %all-gather.11.cloned.1.call-done) | data formatting | bytes 6553600
  306.5 6.5 %convolution_convert_fusion = bf16[128,1280]{1,0:T(8,128)(2,1)} fusion(bf16[1280,1280]{1,0:T(8,128)(2,1)} %reshape.398, bf16[1280,1280]{1,0:T(8,128)(2,1)} %reshape.396, bf16[128,1280]{1,0:T(8,128)(2,1)S(1)} %get-tuple-element.96, f32[1280]{0:T(1024)S(1)} %copy-done.5, f32[128]{0:T(128)S(1)} %add_rsqrt_fusion.2, f32[128]{0:T(128)S(1)} %broadcast_multiply_fusion.1), kind=kOutput, calls=%fused_computation.4 | convolution fusion | flops 850493440 | bytes 7215104 | tf_op jit(solution)/shard_map/dot_general | solution.py:83
  314.2 1.3 dynamic-slice
  315.5 0.7 add_dynamic-update-slice_fusion
  316.2 19.5 %all-reduce = s32[128]{0:T(128)S(1)} all-reduce(s32[128]{0:T(128)S(1)} %add_dynamic-update-slice_fusion), channel_id=2, replica_groups=mesh['tm'=128,'mod'=4] {'tm'}, use_global_device_ids=true, to_apply=%add | all-reduce | flops 128 | bytes 1024
  335.8 157.1 %while.13 = (s32[]{:T(128)}, s32[1]{0:T(128)}, s32[]{:T(128)}, s32[128,1]{0,1:T(1,128)S(1)}, s32[]{:T(128)}) while((s32[]{:T(128)}, s32[1]{0:T(128)}, s32[]{:T(128)}, s32[128,1]{0,1:T(1,128)S(1)}, s32[]{:T(128)}) %tuple.41), condition=%wide.region_1.2_spmd, body=%wide.region_0.1_spmd.sunk | while | flops 5 | bytes 107 | solution.py:20
  337.0 0.6 constant_dynamic-slice_fusion.2
  338.2 0.6 constant_dynamic-slice_fusion.2
  339.5 0.6 constant_dynamic-slice_fusion.2
  340.7 0.6 constant_dynamic-slice_fusion.2
  342.0 0.6 constant_dynamic-slice_fusion.2
  343.2 0.6 constant_dynamic-slice_fusion.2
  344.4 0.6 constant_dynamic-slice_fusion.2
  345.7 0.6 constant_dynamic-slice_fusion.2
  348.1 0.6 constant_dynamic-slice_fusion.2
  350.6 0.6 constant_dynamic-slice_fusion.2
  353.1 0.6 constant_dynamic-slice_fusion.2
  355.6 0.6 constant_dynamic-slice_fusion.2
  358.0 0.6 constant_dynamic-slice_fusion.2
  363.0 0.6 constant_dynamic-slice_fusion.2
  365.5 0.6 constant_dynamic-slice_fusion.2
  371.7 0.6 constant_dynamic-slice_fusion.2
  380.3 0.6 constant_dynamic-slice_fusion.2
  386.5 0.6 constant_dynamic-slice_fusion.2
  389.0 0.6 constant_dynamic-slice_fusion.2
  395.2 0.6 constant_dynamic-slice_fusion.2
  400.1 0.6 constant_dynamic-slice_fusion.2
  413.7 0.6 constant_dynamic-slice_fusion.2
  419.9 0.6 constant_dynamic-slice_fusion.2
  422.4 0.6 constant_dynamic-slice_fusion.2
  428.6 0.6 constant_dynamic-slice_fusion.2
  437.2 0.6 constant_dynamic-slice_fusion.2
  443.4 0.6 constant_dynamic-slice_fusion.2
  445.9 0.6 constant_dynamic-slice_fusion.2
  452.1 0.6 constant_dynamic-slice_fusion.2
  465.7 0.6 constant_dynamic-slice_fusion.2
  471.9 0.6 constant_dynamic-slice_fusion.2
  474.4 0.6 constant_dynamic-slice_fusion.2
  480.5 0.6 constant_dynamic-slice_fusion.2
  486.7 0.6 constant_dynamic-slice_fusion.2
  492.9 1.2 compare_select_fusion.3
  494.1 16.5 %all-to-all-start = ((s32[128,1,1]{2,1,0:T(1,128)}), s32[128,1,1]{2,1,0:T(1,128)S(1)}, u32[]{:S(2)}, u32[]{:S(2)}) async-start(s32[128,1,1]{2,1,0:T(1,128)} %compare_select_fusion.3), calls=%async_computation | async-start | bytes 131072 | tf_op jit(solution)/shard_map/all_to_all | solution.py:118
  511.4 2.5 fusion.89
  513.9 1.2 gather_fusion
  515.2 1.0 convert_add_fusion
  516.7 0.8 reduce_sum.57
  518.3 3.5 convolution_convert_fusion.2
  521.9 0.8 gather_fusion.1
  523.4 0.7 reduce.3
  524.1 0.8 reshape.405
  524.9 16.1 %all-to-all-start.1 = ((bf16[128,2,224]{2,1,0:T(2,128)(2,1)}), bf16[128,2,224]{2,1,0:T(2,128)(2,1)S(1)}, u32[]{:S(2)}, u32[]{:S(2)}) async-start(bf16[128,2,224]{2,1,0:T(2,128)(2,1)} %reshape.405), calls=%async_computation.1 | async-start | bytes 262144 | tf_op jit(solution)/shard_map/all_to_all | solution.py:117
  541.0 2.4 reduce
  543.4 14.7 %all-to-all-done.1 = bf16[128,2,224]{2,1,0:T(2,128)(2,1)S(1)} async-done(((bf16[128,2,224]{2,1,0:T(2,128)(2,1)}), bf16[128,2,224]{2,1,0:T(2,128)(2,1)S(1)}, u32[]{:S(2)}, u32[]{:S(2)}) %all-to-all-start.1) | async-done | bytes 114720 | tf_op jit(solution)/shard_map/all_to_all | solution.py:117
  558.3 1.6 scatter_custom_fusion
  (138 shorter events, 59.1 us)
Async XLA Ops:
  6.5 511.3 %copy-start = (bf16[1280,448]{0,1:T(8,128)(2,1)S(1)}, bf16[1280,448]{0,1:T(8,128)(2,1)}, u32[]{:S(2)}) copy-start(bf16[1280,448]{0,1:T(8,128)(2,1)} %param.20) | copy-start | bytes 3440644
  6.5 151.3 %all-gather.9.cloned.1.call-start = ((), (), s32[]{:S(2)}) async-start(), calls=%async_computation.4 | async-start | bytes 5283840 | tf_op jit(solution)/shard_map/all_gather | solution.py:79
  7.3 292.1 %all-gather.11.cloned.1.call-start = ((), (), s32[]{:S(2)}) async-start(), calls=%async_computation.5 | async-start | bytes 5283840 | tf_op jit(solution)/shard_map/all_gather | solution.py:82
  8.0 507.2 %all-reduce.3.cloned.1.call-start = ((), (), s32[]{:S(2)}) async-start(), calls=%async_computation.3 | async-start | bytes 655360 | tf_op jit(solution)/shard_map/psum | solution.py:84
  8.8 5.7 %collective-permute-start = (bf16[1,128]{1,0:T(2,128)(2,1)S(1)}, bf16[1,128]{1,0:T(2,128)(2,1)S(1)}, u32[]{:S(2)}, u32[]{:S(2)}) collective-permute-start(bf16[1,128]{1,0:T(2,128)(2,1)S(1)} %get-tuple-element.93), channel_id=1, source_target_pairs={{0,4},{4,8},{8,12},{12,16},{16,20},{20,24},{24,28},{28,32},{32,36}... | collective-permute-start | bytes 776 | tf_op jit(solution)/shard_map/ppermute | solution.py:30
  12.5 4.9 collective-permute-start.1
  164.9 141.6 %copy-start.5 = (f32[1280]{0:T(1024)S(1)}, f32[1280]{0:T(1024)}, u32[]{:S(2)}) copy-start(f32[1280]{0:T(1024)} %param.16) | copy-start | bytes 15364
  306.5 204.1 %copy-start.2 = (bf16[256,1280]{1,0:T(8,128)(2,1)S(1)}, bf16[256,1280]{1,0:T(8,128)(2,1)}, u32[]{:S(2)}) copy-start(bf16[256,1280]{1,0:T(8,128)(2,1)} %param.21) | copy-start | bytes 1966084
  306.5 204.3 %copy-start.3 = (f32[1280]{0:T(1024)S(1)}, f32[1280]{0:T(1024)}, u32[]{:S(2)}) copy-start(f32[1280]{0:T(1024)} %param.22) | copy-start | bytes 15364
  313.0 200.9 %copy-start.1 = (s32[1,64]{1,0:T(1,128)S(1)}, s32[1,64]{1,0:T(1,128)}, u32[]{:S(2)}) copy-start(s32[1,64]{1,0:T(1,128)} %param.24) | copy-start | bytes 772
  313.0 205.3 %all-gather.7.cloned.1.call-start = ((), (), s32[]{:S(2)}) async-start(), calls=%async_computation.2 | async-start | bytes 5283840 | tf_op jit(solution)/shard_map/all_gather | solution.py:92
  494.1 30.8 %all-to-all-start = ((s32[128,1,1]{2,1,0:T(1,128)}), s32[128,1,1]{2,1,0:T(1,128)S(1)}, u32[]{:S(2)}, u32[]{:S(2)}) async-start(s32[128,1,1]{2,1,0:T(1,128)} %compare_select_fusion.3), calls=%async_computation | async-start | bytes 131072 | tf_op jit(solution)/shard_map/all_to_all | solution.py:118
  511.0 6.8 %copy-start.4 = (f32[1280]{0:T(1024)S(1)}, f32[1280]{0:T(1024)}, u32[]{:S(2)}) copy-start(f32[1280]{0:T(1024)} %param.19) | copy-start | bytes 15364
  524.9 33.2 %all-to-all-start.1 = ((bf16[128,2,224]{2,1,0:T(2,128)(2,1)}), bf16[128,2,224]{2,1,0:T(2,128)(2,1)S(1)}, u32[]{:S(2)}, u32[]{:S(2)}) async-start(bf16[128,2,224]{2,1,0:T(2,128)(2,1)} %reshape.405), calls=%async_computation.1 | async-start | bytes 262144 | tf_op jit(solution)/shard_map/all_to_all | solution.py:117
Sparse Core Ops, SparseCore 0:
  10.5 147.3 all-gather.8
  161.0 138.3 all-gather.10
  313.1 50.4 all-reduce.2
  366.6 146.1 all-gather.6
where the time goes:
time: 574 us; the launch traced here: 566 us
  waiting for transfers between devices  291 us (51%)
  local copies, waits for them, and re-layouts  97.5 us (17%)
  loops' own time  81.7 us (14%)
  starting transfers between devices  38.4 us (7%)
  blocking collectives  19.5 us (3%)
  between operations  14 us (2%)
  matrix products  13.5 us (2%)
  other arithmetic  10.4 us (2%)
    all_gather x1, waiting for transfers between devices, on_device(): up_share = lax.all_gather(up_weight, 'tm', axis=0, tiled=True)  137 us
    all_gather x1, waiting for transfers between devices, on_device(): down_share = lax.all_gather(down_weight, 'tm', axis=1, tiled=True)  135 us
    another operation x1, loops' own time, carried_in(): return lax.fori_loop(0, count - 1, hop, running)  81.7 us
    dynamic_slice x127, local copies, waits for them, and re-layouts, hop(): longer = join(running, pieces[position])  75.4 us
    unnamed x1, blocking collectives  19.5 us
    all_to_all x1, starting transfers between devices, on_device(): lax.all_to_all(send_slots, 'tm', split_axis=0, concat_axis=0, tiled=True)  16.5 us
    unnamed x18, local copies, waits for them, and re-layouts  16.3 us
    all_to_all x1, starting transfers between devices, on_device(): lax.all_to_all(send_rows, 'tm', split_axis=0, concat_axis=0, tiled=True)  16.1 us
  transfers between devices with their start and end apart: 8, of which 4 were waited for; matrix products, arithmetic and copies ran while one was open for 19% of the time, Pallas kernels for 0%

commit v1 on v0

--- a/solution.py
+++ b/solution.py
@@ -76,7 +76,9 @@
     ).astype(jnp.bfloat16)
     residual = stem.astype(jnp.float32)
     hidden = layer_norm(residual, mlp_gain).astype(jnp.bfloat16)
-    up_share = lax.all_gather(up_weight, "tm", axis=0, tiled=True)
+    up_share = jnp.concatenate(
+        lax.all_to_all(jnp.stack([up_weight] * lax.axis_size("tm")), "tm", 0, 0), axis=0
+    )
     pre_act = jnp.dot(hidden, up_share, preferred_element_type=jnp.float32)
     activated = jax.nn.gelu(pre_act, approximate=False).astype(jnp.bfloat16)
     down_share = lax.all_gather(down_weight, "tm", axis=1, tiled=True)

time: 574 us -> 616 us (1.073)
  blocking collectives: 19.5 us -> 247 us
  waiting for transfers between devices: 291 us -> 68.9 us
  starting transfers between devices: 38.4 us -> 63.2 us
  local copies, waits for them, and re-layouts: 97.5 us -> 108 us
  loops' own time: 81.7 us -> 88.9 us
    unnamed x1, blocking collectives: 19.5 us -> 247 us
    all_gather x1 -> x0, waiting for transfers between devices: 137 us -> none  [on_device(): up_share = lax.all_gather(up_weight, 'tm', axis=0, tiled=True)]
    all_gather x1, waiting for transfers between devices: 135 us -> 0.02 us  [on_device(): down_share = lax.all_gather(down_weight, 'tm', axis=1, tiled=True)]
    psum x1, waiting for transfers between devices: 0.02 us -> 52.7 us  [on_device(): lax.psum(partial_value.astype(jnp.bfloat16), 'mod').astype(jnp.float32)]
    all_to_all x0 -> x1, starting transfers between devices: none -> 20 us  [on_device(): lax.all_to_all(jnp.stack([up_weight] * lax.axis_size('tm')), 'tm', 0, 0)]
    dynamic_slice x127, local copies, waits for them, and re-layouts: 75.4 us -> 83.4 us  [hop(): longer = join(running, pieces[position])]
    another operation x1, loops' own time: 81.7 us -> 88.9 us  [carried_in(): return lax.fori_loop(0, count - 1, hop, running)]
    reshape x0 -> x1, local copies, waits for them, and re-layouts: none -> 7.02 us  [on_device(): jnp.concatenate(lax.all_to_all(jnp.stack([up_weight] * lax.axis_size('tm'...]
  transfers between devices with their start and end apart: 8 -> 8, of which waited for: 4 -> 2; matrix products, arithmetic and copies ran while one was open for 19% -> 21% of each run, Pallas kernels for 0% -> 0%
where the time goes in v1:
time: 616 us; the launch traced here: 614 us
  blocking collectives  247 us (40%)
  local copies, waits for them, and re-layouts  108 us (18%)
  loops' own time  88.9 us (14%)
  waiting for transfers between devices  68.9 us (11%)
  starting transfers between devices  63.2 us (10%)
  between operations  14 us (2%)
  matrix products  13.3 us (2%)
  other arithmetic  10.5 us (2%)
    unnamed x1, blocking collectives  247 us
    another operation x1, loops' own time, carried_in(): return lax.fori_loop(0, count - 1, hop, running)  88.9 us
    dynamic_slice x127, local copies, waits for them, and re-layouts, hop(): longer = join(running, pieces[position])  83.4 us
    psum x1, waiting for transfers between devices, on_device(): lax.psum(partial_value.astype(jnp.bfloat16), 'mod').astype(jnp.float32)  52.7 us
    all_to_all x1, starting transfers between devices, on_device(): lax.all_to_all(jnp.stack([up_weight] * lax.axis_size('tm')), 'tm', 0, 0)  20 us
    all_to_all x1, starting transfers between devices, on_device(): lax.all_to_all(send_rows, 'tm', split_axis=0, concat_axis=0, tiled=True)  18.9 us
    all_to_all x1, starting transfers between devices, on_device(): lax.all_to_all(send_slots, 'tm', split_axis=0, concat_axis=0, tiled=True)  18.8 us
    all_to_all x1, waiting for transfers between devices, on_device(): lax.all_to_all(send_rows, 'tm', split_axis=0, concat_axis=0, tiled=True)  14.7 us
  transfers between devices with their start and end apart: 8, of which 2 were waited for; matrix products, arithmetic and copies ran while one was open for 21% of the time, Pallas kernels for 0%

profile of v1, /device:TPU:33, one launch (start us, length us, event | category | flops | bytes accessed | tf_op | source)
XLA Modules:
  0.0 614.2 jit_solution(17638119141574757490)
XLA Ops:
  6.5 0.7 all-gather.7.cloned.1.call-update
  7.3 3.4 stack.2
  10.6 20.0 %all-to-all-start.1 = ((bf16[128,10,1280]{2,1,0:T(8,128)(2,1)}), bf16[128,10,1280]{2,1,0:T(8,128)(2,1)}, u32[]{:S(2)}, u32[]{:S(2)}) async-start(bf16[128,10,1280]{2,1,0:T(8,128)(2,1)} %stack.2), calls=%async_computation.1 | async-start | bytes 10485760 | tf_op jit(solution)/shard_map/all_to_all | solution.py:80
  30.7 0.7 all-gather.5.cloned.1.call-update
  31.4 3.4 collective-permute-start
  34.8 1.9 collective-permute-start.1
  37.4 1.3 dynamic-slice
  38.7 0.8 add_dynamic-update-slice_fusion
  39.5 247.2 %all-reduce = s32[128]{0:T(128)S(1)} all-reduce(s32[128]{0:T(128)S(1)} %add_dynamic-update-slice_fusion), channel_id=2, replica_groups=mesh['tm'=128,'mod'=4] {'tm'}, use_global_device_ids=true, to_apply=%add | all-reduce | flops 128 | bytes 1024
  286.7 172.2 %while.13 = (s32[]{:T(128)}, s32[1]{0:T(128)}, s32[]{:T(128)}, s32[128,1]{0,1:T(1,128)S(1)}, s32[]{:T(128)}) while((s32[]{:T(128)}, s32[1]{0:T(128)}, s32[]{:T(128)}, s32[128,1]{0,1:T(1,128)S(1)}, s32[]{:T(128)}) %tuple.39), condition=%wide.region_1.2_spmd, body=%wide.region_0.1_spmd.sunk | while | flops 5 | bytes 107 | solution.py:20
  288.0 0.7 constant_dynamic-slice_fusion.2
  289.4 0.7 constant_dynamic-slice_fusion.2
  290.8 0.7 constant_dynamic-slice_fusion.2
  293.5 0.7 constant_dynamic-slice_fusion.2
  294.8 0.7 constant_dynamic-slice_fusion.2
  296.2 0.7 constant_dynamic-slice_fusion.2
  297.5 0.7 constant_dynamic-slice_fusion.2
  300.3 0.7 constant_dynamic-slice_fusion.2
  301.6 0.7 constant_dynamic-slice_fusion.2
  303.0 0.7 constant_dynamic-slice_fusion.2
  304.3 0.7 constant_dynamic-slice_fusion.2
  308.4 0.7 constant_dynamic-slice_fusion.2
  309.7 0.7 constant_dynamic-slice_fusion.2
  311.1 0.7 constant_dynamic-slice_fusion.2
  312.5 0.7 constant_dynamic-slice_fusion.2
  315.2 0.7 constant_dynamic-slice_fusion.2
  316.5 0.7 constant_dynamic-slice_fusion.2
  317.9 0.7 constant_dynamic-slice_fusion.2
  319.2 0.7 constant_dynamic-slice_fusion.2
  322.0 0.7 constant_dynamic-slice_fusion.2
  323.3 0.7 constant_dynamic-slice_fusion.2
  324.7 0.7 constant_dynamic-slice_fusion.2
  326.0 0.7 constant_dynamic-slice_fusion.2
  330.1 0.7 constant_dynamic-slice_fusion.2
  332.8 0.7 constant_dynamic-slice_fusion.2
  334.2 0.7 constant_dynamic-slice_fusion.2
  336.9 0.7 constant_dynamic-slice_fusion.2
  338.2 0.7 constant_dynamic-slice_fusion.2
  339.6 0.7 constant_dynamic-slice_fusion.2
  342.3 0.7 constant_dynamic-slice_fusion.2
  343.7 0.7 constant_dynamic-slice_fusion.2
  345.0 0.7 constant_dynamic-slice_fusion.2
  346.4 0.7 constant_dynamic-slice_fusion.2
  349.1 0.7 constant_dynamic-slice_fusion.2
  350.4 0.7 constant_dynamic-slice_fusion.2
  458.9 2.5 fusion.89
  461.4 1.2 gather_fusion
  462.7 1.2 compare_select_fusion.3
  464.8 2.9 convert_reduce_fusion
  468.0 7.0 %reshape.402 = bf16[1280,1280]{1,0:T(8,128)(2,1)} reshape(bf16[128,10,1280]{2,1,0:T(8,128)(2,1)} %all-gather.7.cloned.1.call-done) | data formatting | bytes 6553600
  475.0 18.8 %all-to-all-start = ((s32[128,1,1]{2,1,0:T(1,128)}), s32[128,1,1]{2,1,0:T(1,128)S(1)}, u32[]{:S(2)}, u32[]{:S(2)}) async-start(s32[128,1,1]{2,1,0:T(1,128)} %compare_select_fusion.3), calls=%async_computation | async-start | bytes 131072 | tf_op jit(solution)/shard_map/all_to_all | solution.py:120
  494.0 7.0 %reshape.369 = bf16[1280,1280]{1,0:T(8,128)(2,1)} reshape(bf16[128,10,1280]{2,1,0:T(8,128)(2,1)} %all-to-all-done.1) | data formatting | bytes 6553600 | tf_op jit(solution)/shard_map/reshape | solution.py:79
  501.0 6.4 %convolution_convert_fusion = bf16[128,1280]{1,0:T(8,128)(2,1)} fusion(bf16[1280,1280]{1,0:T(8,128)(2,1)} %reshape.402, bf16[1280,1280]{1,0:T(8,128)(2,1)} %reshape.369, bf16[128,1280]{1,0:T(8,128)(2,1)S(1)} %get-tuple-element.96, f32[1280]{0:T(1024)S(1)} %copy-done.6, f32[128]{0:T(128)S(1)} %add_rsqrt_fusion.2, f32[128]{0:T(128)S(1)} %broadcast_multiply_fusion.1), kind=kOutput, calls=%fused_computation.4 | convolution fusion | flops 850493440 | bytes 7215104 | tf_op jit(solution)/shard_map/dot_general | solution.py:85
  507.5 3.5 convolution_convert_fusion.2
  511.0 52.7 %all-reduce.3.cloned.1.call-done = bf16[128,1280]{1,0:T(8,128)(2,1)} async-done(((bf16[128,1280]{1,0:T(8,128)(2,1)}), bf16[128,1280]{1,0:T(8,128)(2,1)}) %all-reduce.3.cloned.1.call-update) | async-done | bytes 327696 | tf_op jit(solution)/shard_map/psum | solution.py:86
  563.7 1.0 convert_add_fusion
  565.2 0.8 reduce_sum.57
  566.8 0.8 gather_fusion.1
  568.3 0.7 reduce.3
  569.1 0.8 reshape.409
  569.8 18.9 %all-to-all-start.2 = ((bf16[128,2,224]{2,1,0:T(2,128)(2,1)}), bf16[128,2,224]{2,1,0:T(2,128)(2,1)S(1)}, u32[]{:S(2)}, u32[]{:S(2)}) async-start(bf16[128,2,224]{2,1,0:T(2,128)(2,1)} %reshape.409), calls=%async_computation.2 | async-start | bytes 262144 | tf_op jit(solution)/shard_map/all_to_all | solution.py:119
  588.7 2.4 reduce
  591.1 14.7 %all-to-all-done.2 = bf16[128,2,224]{2,1,0:T(2,128)(2,1)S(1)} async-done(((bf16[128,2,224]{2,1,0:T(2,128)(2,1)}), bf16[128,2,224]{2,1,0:T(2,128)(2,1)S(1)}, u32[]{:S(2)}, u32[]{:S(2)}) %all-to-all-start.2) | async-done | bytes 114720 | tf_op jit(solution)/shard_map/all_to_all | solution.py:119
  606.0 1.6 scatter_custom_fusion
  (140 shorter events, 64.0 us)
Async XLA Ops:
  6.5 559.7 %copy-start = (bf16[1280,448]{0,1:T(8,128)(2,1)S(1)}, bf16[1280,448]{0,1:T(8,128)(2,1)}, u32[]{:S(2)}) copy-start(bf16[1280,448]{0,1:T(8,128)(2,1)} %param.20) | copy-start | bytes 3440644
  6.5 461.4 %all-gather.7.cloned.1.call-start = ((), (), s32[]{:S(2)}) async-start(), calls=%async_computation.5 | async-start | bytes 5283840 | tf_op jit(solution)/shard_map/all_gather | solution.py:84
  10.6 20.8 %copy-start.5 = (bf16[128,128]{1,0:T(8,128)(2,1)S(1)}, bf16[128,128]{1,0:T(8,128)(2,1)}, u32[]{:S(2)}) copy-start(bf16[128,128]{1,0:T(8,128)(2,1)} %param.14) | copy-start | bytes 98308
  10.6 450.8 %copy-start.1 = (s32[1,64]{1,0:T(1,128)S(1)}, s32[1,64]{1,0:T(1,128)}, u32[]{:S(2)}) copy-start(s32[1,64]{1,0:T(1,128)} %param.24) | copy-start | bytes 772
  10.6 453.2 %copy-start.2 = (bf16[256,1280]{1,0:T(8,128)(2,1)S(1)}, bf16[256,1280]{1,0:T(8,128)(2,1)}, u32[]{:S(2)}) copy-start(bf16[256,1280]{1,0:T(8,128)(2,1)} %param.21) | copy-start | bytes 1966084
  10.6 453.5 %copy-start.3 = (f32[1280]{0:T(1024)S(1)}, f32[1280]{0:T(1024)}, u32[]{:S(2)}) copy-start(f32[1280]{0:T(1024)} %param.22) | copy-start | bytes 15364
  10.6 464.4 %all-to-all-start.1 = ((bf16[128,10,1280]{2,1,0:T(8,128)(2,1)}), bf16[128,10,1280]{2,1,0:T(8,128)(2,1)}, u32[]{:S(2)}, u32[]{:S(2)}) async-start(bf16[128,10,1280]{2,1,0:T(8,128)(2,1)} %stack.2), calls=%async_computation.1 | async-start | bytes 10485760 | tf_op jit(solution)/shard_map/all_to_all | solution.py:80
  30.6 476.9 %all-gather.5.cloned.1.call-start = ((), (), s32[]{:S(2)}) async-start(), calls=%async_computation.3 | async-start | bytes 5283840 | tf_op jit(solution)/shard_map/all_gather | solution.py:94
  31.4 433.3 %collective-permute-start = (bf16[1,128]{1,0:T(2,128)(2,1)S(1)}, bf16[1,128]{1,0:T(2,128)(2,1)S(1)}, u32[]{:S(2)}, u32[]{:S(2)}) collective-permute-start(bf16[1,128]{1,0:T(2,128)(2,1)S(1)} %get-tuple-element.93), channel_id=1, source_target_pairs={{0,4},{4,8},{8,12},{12,16},{16,20},{20,24},{24,28},{28,32},{32,36}... | collective-permute-start | bytes 776 | tf_op jit(solution)/shard_map/ppermute | solution.py:30
  34.8 430.0 %collective-permute-start.1 = (bf16[1,128]{1,0:T(2,128)(2,1)S(1)}, bf16[1,128]{1,0:T(2,128)(2,1)S(1)}, u32[]{:S(2)}, u32[]{:S(2)}) collective-permute-start(bf16[1,128]{1,0:T(2,128)(2,1)S(1)} %get-tuple-element.94), channel_id=1, source_target_pairs={{4,0},{8,4},{12,8},{16,12},{20,16},{24,20},{28,24},{32,28},{36,32}... | collective-permute-start | bytes 776 | tf_op jit(solution)/shard_map/ppermute | solution.py:31
  475.0 94.8 %all-to-all-start = ((s32[128,1,1]{2,1,0:T(1,128)}), s32[128,1,1]{2,1,0:T(1,128)S(1)}, u32[]{:S(2)}, u32[]{:S(2)}) async-start(s32[128,1,1]{2,1,0:T(1,128)} %compare_select_fusion.3), calls=%async_computation | async-start | bytes 131072 | tf_op jit(solution)/shard_map/all_to_all | solution.py:120
  493.8 7.3 %copy-start.6 = (f32[1280]{0:T(1024)S(1)}, f32[1280]{0:T(1024)}, u32[]{:S(2)}) copy-start(f32[1280]{0:T(1024)} %param.16) | copy-start | bytes 15364
  493.8 69.9 %all-reduce.3.cloned.1.call-start = ((), (), s32[]{:S(2)}) async-start(), calls=%async_computation.4 | async-start | bytes 655360 | tf_op jit(solution)/shard_map/psum | solution.py:86
  511.0 55.3 %copy-start.4 = (f32[1280]{0:T(1024)S(1)}, f32[1280]{0:T(1024)}, u32[]{:S(2)}) copy-start(f32[1280]{0:T(1024)} %param.19) | copy-start | bytes 15364
  569.8 36.0 %all-to-all-start.2 = ((bf16[128,2,224]{2,1,0:T(2,128)(2,1)}), bf16[128,2,224]{2,1,0:T(2,128)(2,1)S(1)}, u32[]{:S(2)}, u32[]{:S(2)}) async-start(bf16[128,2,224]{2,1,0:T(2,128)(2,1)} %reshape.409), calls=%async_computation.2 | async-start | bytes 262144 | tf_op jit(solution)/shard_map/all_to_all | solution.py:119
Sparse Core Ops, SparseCore 0:
  10.5 185.3 all-gather.6
  199.0 160.9 all-gather.4
  507.6 56.0 all-reduce.2
